TPU v7x, 256 devices: a whole 4x4x8 slice. The times are simulated.
256 devices in a mesh: roll: 64 (over z, y_lo, x), tp: 4 (over y_hi, core).
Axes of the slice: x: 4, y: 4 (y_hi: 2, y_lo: 2; y = y_hi * 2 + y_lo), z: 8, core: 2. Of those that a mesh axis runs over, the one named last changes fastest.
Arguments:
- hidden_in: bfloat16 [8192, 5120], P('roll', 'tp'), may hold values from -480 to 480
- qkv_weight: bfloat16 [5120, 3584], P('roll', 'tp'), may hold values from -1 to 1
- sample_group: int32 [8192], P('roll'), may hold values from 0 to 127, as said below
- prefix_blocks: int32 [128], P('roll'), may hold values from 1 to 4, as said below
- prefix_kv: bfloat16 [128, 512, 1024], P('roll', None, 'tp'), may hold values from -24 to 24
- page_table: int32 [8192, 2], P('roll'), may hold values from 0 to 255, as said below
- suffix_pool: bfloat16 [16384, 16, 1024], P('roll', None, 'tp'), may hold values from -24 to 24
Outputs:
- attended: bfloat16 [8192, 2560], P('roll', 'tp')
Inputs may be any that keep to these rules, and one draw needn't show every extreme that they name: `sample_group`: on each index of roll the 128 entries name every group exactly once. `prefix_blocks`: some group has exactly 4 blocks. `page_table`: on each index of roll the entries are a permutation of 0 to 255.
All inputs are finite; a program needn't handle non-finite values.
Results may differ from a plain program's by a relative error of at most 0.0096.
Values may be sent and summed in bfloat16 or wider, within the bound.
A program may use at most 64 MiB of HBM per device.

v0:
```python
import math
import jax
import jax.numpy as jnp
from jax import lax
from jax.sharding import PartitionSpec as P

HEADS = 20
KV_HEADS = 4
HD = 128
BLOCK = 128
PAGE = 16
SPAGES = 2
MASKED = -1e30


def softmax_parts(scores):
    row_max = jnp.max(scores, axis=-1)
    exponent = jnp.exp(scores - row_max[..., None])
    row_sum = jnp.sum(exponent, axis=-1)
    return (exponent, row_max, row_sum)


def merge_parts(first_out, first_lse, second_out, second_lse):
    combined = jnp.logaddexp(first_lse, second_lse)
    mixed = (
        jnp.exp(first_lse - combined)[..., None] * first_out
        + jnp.exp(second_lse - combined)[..., None] * second_out
    )
    return mixed.astype(jnp.bfloat16)


def per_device(
    hidden_in, qkv_weight, sample_group, prefix_blocks, prefix_kv, page_table, suffix_pool
):
    whole = lax.all_gather(hidden_in, "tp", axis=1, tiled=True)
    row_count = whole.shape[0]
    kv_heads_dev = prefix_kv.shape[2] // (2 * HD)
    repeat = HEADS // KV_HEADS
    q_width = kv_heads_dev * repeat * HD
    head_count = kv_heads_dev * repeat
    owned_groups = prefix_kv.shape[0]
    roll_count = lax.axis_size("roll")
    per_group = row_count // (roll_count * owned_groups)
    owner_rows = roll_count * per_group
    prefix_span = prefix_kv.shape[1]
    score_scale = 1.0 / math.sqrt(HD)
    float_in = whole.astype(jnp.float32)
    normed = (
        float_in * lax.rsqrt(jnp.mean(float_in * float_in, axis=-1, keepdims=True) + 1e-06)
    ).astype(jnp.bfloat16)
    united_proj = jnp.dot(
        normed,
        lax.all_gather(qkv_weight, "roll", axis=0, tiled=True),
        preferred_element_type=jnp.float32,
    )
    united_proj = united_proj.astype(jnp.bfloat16).reshape(row_count, kv_heads_dev, repeat + 2, HD)
    queries = united_proj[:, :, :repeat]
    own_key = united_proj[:, :, repeat]
    own_value = united_proj[:, :, repeat + 1]
    sort_order = jnp.argsort(sample_group, stable=True)

    def sample_layout(arrived, width, dtype):
        return (
            jnp.zeros((row_count, width), dtype)
            .at[sort_order]
            .set(arrived.reshape(row_count, width))
        )

    page_rows = suffix_pool[page_table].reshape(row_count, SPAGES * PAGE, kv_heads_dev, 2, HD)
    key_rows = jnp.concatenate([page_rows[:, :, :, 0], own_key[:, None]], axis=1)
    value_rows = jnp.concatenate([page_rows[:, :, :, 1], own_value[:, None]], axis=1)
    scores = (
        jnp.einsum("sjrd,stjd->sjrt", queries, key_rows, preferred_element_type=jnp.float32)
        * score_scale
    )
    exponent, row_max, row_sum = softmax_parts(scores)
    weights = (exponent / row_sum[..., None]).astype(jnp.bfloat16)
    result = jnp.einsum("sjrt,stjd->sjrd", weights, value_rows, preferred_element_type=jnp.float32)
    local_out = result
    local_lse = row_max + jnp.log(row_sum)
    incoming = lax.all_to_all(
        queries.reshape(row_count, q_width)[sort_order].reshape(
            roll_count, owned_groups, per_group, q_width
        ),
        "roll",
        split_axis=0,
        concat_axis=2,
        tiled=True,
    )
    kv_cache = prefix_kv.reshape(owned_groups, prefix_span, kv_heads_dev, 2, HD)
    scores = (
        jnp.einsum(
            "gqjrd,gtjd->gqjrt",
            incoming.reshape(owned_groups, owner_rows, kv_heads_dev, repeat, HD),
            kv_cache[:, :, :, 0],
            preferred_element_type=jnp.float32,
        )
        * score_scale
    )
    live_mask = (jnp.arange(prefix_span)[None, :] < prefix_blocks[:, None] * BLOCK)[
        :, None, None, None, :
    ]
    scores = jnp.where(live_mask, scores, MASKED)
    row_max = jnp.max(scores, axis=-1)
    exponent = jnp.where(live_mask, jnp.exp(scores - row_max[..., None]), 0.0)
    row_sum = jnp.sum(exponent, axis=-1)
    weights = (exponent / row_sum[..., None]).astype(jnp.bfloat16)
    result = jnp.einsum(
        "gqjrt,gtjd->gqjrd", weights, kv_cache[:, :, :, 1], preferred_element_type=jnp.float32
    )
    result, result_lse = (result, row_max + jnp.log(row_sum))
    back_out = lax.all_to_all(
        result.reshape(1, owned_groups, owner_rows, q_width),
        "roll",
        split_axis=2,
        concat_axis=0,
        tiled=True,
    )
    back_lse = lax.all_to_all(
        result_lse.reshape(1, owned_groups, owner_rows, head_count),
        "roll",
        split_axis=2,
        concat_axis=0,
        tiled=True,
    )
    prefix_out = sample_layout(back_out, q_width, jnp.float32)
    prefix_lse = sample_layout(back_lse, head_count, jnp.float32)
    prefix_out, prefix_lse = (
        prefix_out.reshape(row_count, kv_heads_dev, repeat, HD),
        prefix_lse.reshape(row_count, kv_heads_dev, repeat),
    )
    return merge_parts(prefix_out, prefix_lse, local_out, local_lse).reshape(row_count, q_width)


def solution(mesh):
    in_specs = (
        P("roll", "tp"),
        P("roll", "tp"),
        P("roll"),
        P("roll"),
        P("roll", None, "tp"),
        P("roll", None),
        P("roll", None, "tp"),
    )
    out_specs = P("roll", "tp")
    return jax.shard_map(
        per_device, mesh=mesh, in_specs=in_specs, out_specs=out_specs, check_vma=False
    )
```

profile of v0, /device:TPU:16, one launch (start us, length us, event | category | flops | bytes accessed | tf_op | source)
XLA Modules:
  0.0 428.6 jit_solution(3843228985545048968)
XLA Ops:
  8.9 2.0 copy.137
  11.0 2.1 gather_fusion.1
  13.1 4.0 reshape.185
  17.1 2.5 sort.17
  19.7 7.5 %fusion.40 = (bf16[128,32,1,1,128]{4,3,1,0,2:T(2,128)(2,1)}, bf16[128,32,1,1,128]{4,3,1,0,2:T(2,128)(2,1)}) fusion(bf16[128,32,1,2,128]{4,3,1,0,2:T(2,128)(2,1)} %reshape.185), kind=kLoop, calls=%fused_computation.69 | loop fusion | bytes 4194304 | tf_op jit(solution)/shard_map/slice | solution.py:70
  27.2 6.8 %all-gather.3.cloned.1.call-done = bf16[128,5120]{1,0:T(8,128)(2,1)} async-done(((bf16[128,1280]{1,0:T(8,128)(2,1)}), bf16[128,5120]{1,0:T(8,128)(2,1)}) %all-gather.3.cloned.1.call-update) | async-done | bytes 1310736 | tf_op jit(solution)/shard_map/all_gather | solution.py:35
  34.1 1.8 fusion
  35.8 316.4 %all-gather.5.cloned.1.call-done = bf16[5120,896]{1,0:T(8,128)(2,1)} async-done(((bf16[80,896]{1,0:T(8,128)(2,1)}), bf16[5120,896]{1,0:T(8,128)(2,1)}) %all-gather.5.cloned.1.call-update) | async-done | bytes 9175056 | tf_op jit(solution)/shard_map/all_gather | solution.py:53
  352.2 5.9 %fusion.19 = bf16[128,896]{1,0:T(8,128)(2,1)} fusion(bf16[5120,896]{1,0:T(8,128)(2,1)} %all-gather.5.cloned.1.call-done, bf16[128,5120]{1,0:T(8,128)(2,1)S(1)} %copy-done.1, f32[128]{0:T(128)S(1)} %add_rsqrt_fusion), kind=kOutput, calls=%fused_computation.30 | convolution fusion | flops 1176485888 | bytes 10715648 | tf_op jit(solution)/shard_map/dot_general | solution.py:51
  358.1 1.1 copy.131
  361.0 8.6 %all-to-all-start = ((bf16[64,2,1,640]{3,1,2,0:T(2,128)(2,1)}), bf16[64,2,1,640]{3,1,2,0:T(2,128)(2,1)S(1)}, u32[]{:S(2)}, u32[]{:S(2)}) async-start(bf16[64,2,1,640]{3,1,2,0:T(2,128)(2,1)} %bitcast.2), calls=%async_computation | async-start | bytes 327680 | tf_op jit(solution)/shard_map/all_to_all | solution.py:81
  369.6 4.1 copy_bitcast_fusion
  373.7 6.9 %all-to-all-done = bf16[64,2,1,640]{3,1,2,0:T(2,128)(2,1)S(1)} async-done(((bf16[64,2,1,640]{3,1,2,0:T(2,128)(2,1)}), bf16[64,2,1,640]{3,1,2,0:T(2,128)(2,1)S(1)}, u32[]{:S(2)}, u32[]{:S(2)}) %all-to-all-start) | async-done | bytes 163872 | tf_op jit(solution)/shard_map/all_to_all | solution.py:81
  381.5 1.4 bitcast_reduce_fusion
  384.1 4.6 %all-to-all-start.1 = ((f32[1,2,64,5]{3,1,0,2:T(2,128)}), f32[1,2,64,5]{3,1,0,2:T(2,128)S(1)}, u32[]{:S(2)}, u32[]{:S(2)}) async-start(f32[1,2,64,5]{3,1,0,2:T(2,128)} %copy.140), calls=%async_computation.1 | async-start | bytes 131072 | tf_op jit(solution)/shard_map/all_to_all | solution.py:119
  388.7 1.5 convolution_bitcast_fusion
  390.4 1.0 reshape.235
  391.3 7.9 %all-to-all-done.1 = f32[1,2,64,5]{3,1,0,2:T(2,128)S(1)} async-done(((f32[1,2,64,5]{3,1,0,2:T(2,128)}), f32[1,2,64,5]{3,1,0,2:T(2,128)S(1)}, u32[]{:S(2)}, u32[]{:S(2)}) %all-to-all-start.1) | async-done | bytes 2592 | tf_op jit(solution)/shard_map/all_to_all | solution.py:119
  399.3 4.6 %all-to-all-start.2 = ((f32[1,2,64,640]{3,1,0,2:T(2,128)}), f32[1,2,64,640]{3,1,0,2:T(2,128)S(1)}, u32[]{:S(2)}, u32[]{:S(2)}) async-start(f32[1,2,64,640]{3,1,0,2:T(2,128)} %reshape.235), calls=%async_computation.2 | async-start | bytes 655360 | tf_op jit(solution)/shard_map/all_to_all | solution.py:112
  405.8 2.2 fusion.42
  410.5 5.8 %all-to-all-done.2 = f32[1,2,64,640]{3,1,0,2:T(2,128)S(1)} async-done(((f32[1,2,64,640]{3,1,0,2:T(2,128)}), f32[1,2,64,640]{3,1,0,2:T(2,128)S(1)}, u32[]{:S(2)}, u32[]{:S(2)}) %all-to-all-start.2) | async-done | bytes 327712 | tf_op jit(solution)/shard_map/all_to_all | solution.py:112
  416.5 1.1 scatter_custom_fusion.1
  417.7 1.0 copy.155
  418.8 2.0 fusion.18
  (53 shorter events, 12.2 us)
Async XLA Ops:
  6.5 4.5 %copy-start = (bf16[256,16,256]{2,1,0:T(8,128)(2,1)S(1)}, bf16[256,16,256]{2,1,0:T(8,128)(2,1)}, u32[]{:S(2)}) copy-start(bf16[256,16,256]{2,1,0:T(8,128)(2,1)} %param.13) | copy-start | bytes 6291460
  6.5 27.5 %all-gather.3.cloned.1.call-start = ((), (), s32[]{:S(2)}) async-start(), calls=%async_computation.3 | async-start | bytes 1638400 | tf_op jit(solution)/shard_map/all_gather | solution.py:35
  7.3 344.9 %all-gather.5.cloned.1.call-start = ((), (), s32[]{:S(2)}) async-start(), calls=%async_computation.4 | async-start | bytes 9318400 | tf_op jit(solution)/shard_map/all_gather | solution.py:53
  13.1 4.0 copy-start.5
  13.1 6.6 %copy-start.6 = (s32[2]{0:T(128)S(1)}, s32[2]{0:T(128)}, u32[]{:S(2)}) copy-start(s32[2]{0:T(128)} %param.10) | copy-start | bytes 28
  34.1 318.1 %copy-start.1 = (bf16[128,5120]{1,0:T(8,128)(2,1)S(1)}, bf16[128,5120]{1,0:T(8,128)(2,1)}, u32[]{:S(2)}) copy-start(bf16[128,5120]{1,0:T(8,128)(2,1)} %all-gather.3.cloned.1.call-done) | copy-start | bytes 3932164
  359.2 1.8 copy-start.4
  359.2 14.5 %copy-start.2 = (bf16[128,1,5,128]{0,3,2,1:T(8,128)(2,1)}, bf16[128,1,5,128]{0,3,2,1:T(8,128)(2,1)S(1)}, u32[]{:S(2)}) copy-start(bf16[128,1,5,128]{0,3,2,1:T(8,128)(2,1)S(1)} %slice.32) | copy-start | bytes 491524
  361.0 19.6 %all-to-all-start = ((bf16[64,2,1,640]{3,1,2,0:T(2,128)(2,1)}), bf16[64,2,1,640]{3,1,2,0:T(2,128)(2,1)S(1)}, u32[]{:S(2)}, u32[]{:S(2)}) async-start(bf16[64,2,1,640]{3,1,2,0:T(2,128)(2,1)} %bitcast.2), calls=%async_computation | async-start | bytes 327680 | tf_op jit(solution)/shard_map/all_to_all | solution.py:81
  384.1 15.2 %all-to-all-start.1 = ((f32[1,2,64,5]{3,1,0,2:T(2,128)}), f32[1,2,64,5]{3,1,0,2:T(2,128)S(1)}, u32[]{:S(2)}, u32[]{:S(2)}) async-start(f32[1,2,64,5]{3,1,0,2:T(2,128)} %copy.140), calls=%async_computation.1 | async-start | bytes 131072 | tf_op jit(solution)/shard_map/all_to_all | solution.py:119
  390.1 14.6 %copy-start.3 = (bf16[128,1,5,128]{0,3,2,1:T(8,128)(2,1)S(1)}, bf16[128,1,5,128]{0,3,2,1:T(8,128)(2,1)}, u32[]{:S(2)}) copy-start(bf16[128,1,5,128]{0,3,2,1:T(8,128)(2,1)} %copy-done.2) | copy-start | bytes 491524
  399.3 17.0 %all-to-all-start.2 = ((f32[1,2,64,640]{3,1,0,2:T(2,128)}), f32[1,2,64,640]{3,1,0,2:T(2,128)S(1)}, u32[]{:S(2)}, u32[]{:S(2)}) async-start(f32[1,2,64,640]{3,1,0,2:T(2,128)} %reshape.235), calls=%async_computation.2 | async-start | bytes 655360 | tf_op jit(solution)/shard_map/all_to_all | solution.py:112
Sparse Core Ops, SparseCore 0:
  9.2 24.8 all-gather.2
  35.9 316.2 all-gather.4
where the time goes:
time: 429 us
  waiting for transfers between devices  345 us (80%)
  local copies, waits for them, and re-layouts  33 us (8%)
  starting transfers between devices  17.9 us (4%)
  between operations  13.6 us (3%)
  matrix products  12.9 us (3%)
  other arithmetic  5.93 us (1%)
    all_gather x1, waiting for transfers between devices, per_device(): lax.all_gather(qkv_weight, 'roll', axis=0, tiled=True)  316 us
    all_to_all x1, starting transfers between devices, per_device(): lax.all_to_all(queries.reshape(row_count, q_width)[sort_order].reshape(ro...  8.61 us
  transfers between devices with their start and end apart: 5, of which 5 were waited for; matrix products, arithmetic and copies ran while one was open for 8% of the time, Pallas kernels for 0%

commit v1 on v0

--- a/solution.py
+++ b/solution.py
@@ -50,7 +50,9 @@
     ).astype(jnp.bfloat16)
     united_proj = jnp.dot(
         normed,
-        lax.all_gather(qkv_weight, "roll", axis=0, tiled=True),
+        jnp.concatenate(
+            lax.all_to_all(jnp.stack([qkv_weight] * lax.axis_size("roll")), "roll", 0, 0), axis=0
+        ),
         preferred_element_type=jnp.float32,
     )
     united_proj = united_proj.astype(jnp.bfloat16).reshape(row_count, kv_heads_dev, repeat + 2, HD)

time: 429 us -> 302 us (0.70)
  waiting for transfers between devices: 345 us -> 203 us
  starting transfers between devices: 17.9 us -> 29.3 us
  local copies, waits for them, and re-layouts: 33 us -> 37.3 us
    all_gather x1 -> x0, waiting for transfers between devices: 316 us -> none  [per_device(): lax.all_gather(qkv_weight, 'roll', axis=0, tiled=True)]
    all_to_all x0 -> x1, waiting for transfers between devices: none -> 158 us  [per_device(): lax.all_to_all(jnp.stack([qkv_weight] * lax.axis_size('roll')), 'roll', 0...]
    all_gather x1, waiting for transfers between devices: 6.83 us -> 23.9 us  [per_device(): whole = lax.all_gather(hidden_in, 'tp', axis=1, tiled=True)]
    all_to_all x0 -> x1, starting transfers between devices: none -> 13 us  [per_device(): lax.all_to_all(jnp.stack([qkv_weight] * lax.axis_size('roll')), 'roll', 0...]
    another operation x1 -> x2, local copies, waits for them, and re-layouts: 0.84 us -> 6.12 us  [the longest x1 5.28 us: per_device(): jnp.stack([qkv_weight] * lax.axis_size('roll'))]
  transfers between devices with their start and end apart: 5 -> 5, of which waited for: 5 -> 5; matrix products, arithmetic and copies ran while one was open for 8% -> 11% of each run, Pallas kernels for 0% -> 0%
where the time goes in v1:
time: 302 us
  waiting for transfers between devices  203 us (67%)
  local copies, waits for them, and re-layouts  37.3 us (12%)
  starting transfers between devices  29.3 us (10%)
  between operations  13.6 us (5%)
  matrix products  12.9 us (4%)
  other arithmetic  5.25 us (2%)
    all_to_all x1, waiting for transfers between devices, per_device(): lax.all_to_all(jnp.stack([qkv_weight] * lax.axis_size('roll')), 'roll', 0...  158 us
    all_gather x1, waiting for transfers between devices, per_device(): whole = lax.all_gather(hidden_in, 'tp', axis=1, tiled=True)  23.9 us
    all_to_all x1, starting transfers between devices, per_device(): lax.all_to_all(jnp.stack([qkv_weight] * lax.axis_size('roll')), 'roll', 0...  13 us
    all_to_all x1, waiting for transfers between devices, per_device(): lax.all_to_all(result_lse.reshape(1, owned_groups, owner_rows, head_count...  7.95 us
    slice x1, local copies, waits for them, and re-layouts, per_device(): page_rows[:, :, :, 0]  7.48 us
    all_to_all x1, waiting for transfers between devices, per_device(): lax.all_to_all(queries.reshape(row_count, q_width)[sort_order].reshape(ro...  7.01 us
    all_to_all x1, starting transfers between devices, per_device(): lax.all_to_all(queries.reshape(row_count, q_width)[sort_order].reshape(ro...  6.86 us
  transfers between devices with their start and end apart: 5, of which 5 were waited for; matrix products, arithmetic and copies ran while one was open for 11% of the time, Pallas kernels for 0%

profile of v1, /device:TPU:16, one launch (start us, length us, event | category | flops | bytes accessed | tf_op | source)
XLA Modules:
  0.0 301.6 jit_solution(840228505978401053)
XLA Ops:
  6.5 5.3 %stack.2 = bf16[64,80,896]{2,1,0:T(8,128)(2,1)} broadcast(bf16[80,896]{1,0:T(8,128)(2,1)} %param.8), dimensions={1,2} | broadcast | bytes 9318400 | tf_op jit(solution)/shard_map/stack | solution.py:54
  11.8 13.0 %all-to-all-start = ((bf16[64,80,896]{2,1,0:T(8,128)(2,1)}), bf16[64,80,896]{2,1,0:T(8,128)(2,1)}, u32[]{:S(2)}, u32[]{:S(2)}) async-start(bf16[64,80,896]{2,1,0:T(8,128)(2,1)} %stack.2), calls=%async_computation | async-start | bytes 18350080 | tf_op jit(solution)/shard_map/all_to_all | solution.py:54
  25.9 2.1 gather_fusion.1
  28.0 4.0 %reshape.191 = bf16[128,32,1,2,128]{4,3,1,0,2:T(2,128)(2,1)} reshape(bf16[256,16,256]{2,1,0:T(8,128)(2,1)} %gather_fusion.1) | data formatting | bytes 4194304 | tf_op jit(solution)/shard_map/reshape | solution.py:71
  32.0 1.0 copy.137
  33.0 2.5 sort.17
  35.7 7.5 %fusion.40 = (bf16[128,32,1,1,128]{4,3,1,0,2:T(2,128)(2,1)}, bf16[128,32,1,1,128]{4,3,1,0,2:T(2,128)(2,1)}) fusion(bf16[128,32,1,2,128]{4,3,1,0,2:T(2,128)(2,1)} %reshape.191), kind=kLoop, calls=%fused_computation.69 | loop fusion | bytes 4194304 | tf_op jit(solution)/shard_map/slice | solution.py:72
  43.1 23.9 %all-gather.2.cloned.1.call-done = bf16[128,5120]{1,0:T(8,128)(2,1)} async-done(((bf16[128,1280]{1,0:T(8,128)(2,1)}), bf16[128,5120]{1,0:T(8,128)(2,1)}) %all-gather.2.cloned.1.call-update) | async-done | bytes 1310736 | tf_op jit(solution)/shard_map/all_gather | solution.py:35
  67.1 1.8 fusion
  68.8 158.0 %all-to-all-done = bf16[64,80,896]{2,1,0:T(8,128)(2,1)} async-done(((bf16[64,80,896]{2,1,0:T(8,128)(2,1)}), bf16[64,80,896]{2,1,0:T(8,128)(2,1)}, u32[]{:S(2)}, u32[]{:S(2)}) %all-to-all-start) | async-done | bytes 9175072 | tf_op jit(solution)/shard_map/all_to_all | solution.py:54
  226.8 5.9 %fusion.19 = bf16[128,896]{1,0:T(8,128)(2,1)} fusion(bf16[5120,896]{1,0:T(8,128)(2,1)} %bitcast, bf16[128,5120]{1,0:T(8,128)(2,1)S(1)} %copy-done.1, f32[128]{0:T(128)S(1)} %add_rsqrt_fusion), kind=kOutput, calls=%fused_computation.30 | convolution fusion | flops 1176485888 | bytes 10715648 | tf_op jit(solution)/shard_map/dot_general | solution.py:51
  232.7 1.1 copy.131
  235.7 6.9 %all-to-all-start.1 = ((bf16[64,2,1,640]{3,1,2,0:T(2,128)(2,1)}), bf16[64,2,1,640]{3,1,2,0:T(2,128)(2,1)S(1)}, u32[]{:S(2)}, u32[]{:S(2)}) async-start(bf16[64,2,1,640]{3,1,2,0:T(2,128)(2,1)} %bitcast.3), calls=%async_computation.1 | async-start | bytes 327680 | tf_op jit(solution)/shard_map/all_to_all | solution.py:83
  242.5 4.1 %copy_bitcast_fusion = (bf16[128,32,1,128]{3,1,0,2:T(8,128)(2,1)}, bf16[128,32,1,128]{3,1,0,2:T(8,128)(2,1)}) fusion(bf16[128,32,1,1,128]{4,3,1,0,2:T(2,128)(2,1)} %get-tuple-element.8, bf16[128,32,1,1,128]{4,3,1,0,2:T(2,128)(2,1)} %get-tuple-element.7), kind=kLoop, calls=%fused_computation.33 | loop fusion | bytes 4194304 | tf_op jit(solution)/shard_map/squeeze | solution.py:73
  246.6 7.0 %all-to-all-done.1 = bf16[64,2,1,640]{3,1,2,0:T(2,128)(2,1)S(1)} async-done(((bf16[64,2,1,640]{3,1,2,0:T(2,128)(2,1)}), bf16[64,2,1,640]{3,1,2,0:T(2,128)(2,1)S(1)}, u32[]{:S(2)}, u32[]{:S(2)}) %all-to-all-start.1) | async-done | bytes 163872 | tf_op jit(solution)/shard_map/all_to_all | solution.py:83
  254.5 1.4 bitcast_reduce_fusion
  257.1 4.6 %all-to-all-start.2 = ((f32[1,2,64,5]{3,1,0,2:T(2,128)}), f32[1,2,64,5]{3,1,0,2:T(2,128)S(1)}, u32[]{:S(2)}, u32[]{:S(2)}) async-start(f32[1,2,64,5]{3,1,0,2:T(2,128)} %copy.140), calls=%async_computation.2 | async-start | bytes 131072 | tf_op jit(solution)/shard_map/all_to_all | solution.py:121
  261.7 1.5 convolution_bitcast_fusion
  264.3 7.9 %all-to-all-done.2 = f32[1,2,64,5]{3,1,0,2:T(2,128)S(1)} async-done(((f32[1,2,64,5]{3,1,0,2:T(2,128)}), f32[1,2,64,5]{3,1,0,2:T(2,128)S(1)}, u32[]{:S(2)}, u32[]{:S(2)}) %all-to-all-start.2) | async-done | bytes 2592 | tf_op jit(solution)/shard_map/all_to_all | solution.py:121
  272.3 4.8 %all-to-all-start.3 = ((f32[1,2,64,640]{3,1,0,2:T(2,128)}), f32[1,2,64,640]{3,1,0,2:T(2,128)S(1)}, u32[]{:S(2)}, u32[]{:S(2)}) async-start(f32[1,2,64,640]{3,1,0,2:T(2,128)} %reshape.241), calls=%async_computation.3 | async-start | bytes 655360 | tf_op jit(solution)/shard_map/all_to_all | solution.py:114
  279.0 2.2 fusion.42
  283.6 5.6 %all-to-all-done.3 = f32[1,2,64,640]{3,1,0,2:T(2,128)S(1)} async-done(((f32[1,2,64,640]{3,1,0,2:T(2,128)}), f32[1,2,64,640]{3,1,0,2:T(2,128)S(1)}, u32[]{:S(2)}, u32[]{:S(2)}) %all-to-all-start.3) | async-done | bytes 327712 | tf_op jit(solution)/shard_map/all_to_all | solution.py:114
  289.5 1.1 scatter_custom_fusion.1
  291.8 2.0 fusion.18
  (57 shorter events, 12.8 us)
Async XLA Ops:
  6.5 19.3 %copy-start = (bf16[256,16,256]{2,1,0:T(8,128)(2,1)S(1)}, bf16[256,16,256]{2,1,0:T(8,128)(2,1)}, u32[]{:S(2)}) copy-start(bf16[256,16,256]{2,1,0:T(8,128)(2,1)} %param.13) | copy-start | bytes 6291460
  11.8 13.8 %copy-start.6 = (s32[128,2]{0,1:T(2,128)S(1)}, s32[128,2]{0,1:T(2,128)}, u32[]{:S(2)}) copy-start(s32[128,2]{0,1:T(2,128)} %param.12) | copy-start | bytes 3076
  11.8 215.0 %all-to-all-start = ((bf16[64,80,896]{2,1,0:T(8,128)(2,1)}), bf16[64,80,896]{2,1,0:T(8,128)(2,1)}, u32[]{:S(2)}, u32[]{:S(2)}) async-start(bf16[64,80,896]{2,1,0:T(8,128)(2,1)} %stack.2), calls=%async_computation | async-start | bytes 18350080 | tf_op jit(solution)/shard_map/all_to_all | solution.py:54
  24.8 42.2 %all-gather.2.cloned.1.call-start = ((), (), s32[]{:S(2)}) async-start(), calls=%async_computation.4 | async-start | bytes 1638400 | tf_op jit(solution)/shard_map/all_gather | solution.py:35
  28.0 4.0 %copy-start.5 = (bf16[2,512,256]{2,1,0:T(8,128)(2,1)S(1)}, bf16[2,512,256]{2,1,0:T(8,128)(2,1)}, u32[]{:S(2)}) copy-start(bf16[2,512,256]{2,1,0:T(8,128)(2,1)} %param.11) | copy-start | bytes 1572868
  28.0 5.1 %copy-start.7 = (s32[128]{0:T(128)S(1)}, s32[128]{0:T(128)}, u32[]{:S(2)}) copy-start(s32[128]{0:T(128)} %param.9) | copy-start | bytes 1540
  28.0 7.6 %copy-start.8 = (s32[2]{0:T(128)S(1)}, s32[2]{0:T(128)}, u32[]{:S(2)}) copy-start(s32[2]{0:T(128)} %param.10) | copy-start | bytes 28
  67.1 159.8 %copy-start.1 = (bf16[128,5120]{1,0:T(8,128)(2,1)S(1)}, bf16[128,5120]{1,0:T(8,128)(2,1)}, u32[]{:S(2)}) copy-start(bf16[128,5120]{1,0:T(8,128)(2,1)} %all-gather.2.cloned.1.call-done) | copy-start | bytes 3932164
  233.8 1.8 copy-start.4
  233.9 12.7 %copy-start.2 = (bf16[128,1,5,128]{0,3,2,1:T(8,128)(2,1)}, bf16[128,1,5,128]{0,3,2,1:T(8,128)(2,1)S(1)}, u32[]{:S(2)}) copy-start(bf16[128,1,5,128]{0,3,2,1:T(8,128)(2,1)S(1)} %slice.32) | copy-start | bytes 491524
  235.7 18.0 %all-to-all-start.1 = ((bf16[64,2,1,640]{3,1,2,0:T(2,128)(2,1)}), bf16[64,2,1,640]{3,1,2,0:T(2,128)(2,1)S(1)}, u32[]{:S(2)}, u32[]{:S(2)}) async-start(bf16[64,2,1,640]{3,1,2,0:T(2,128)(2,1)} %bitcast.3), calls=%async_computation.1 | async-start | bytes 327680 | tf_op jit(solution)/shard_map/all_to_all | solution.py:83
  257.1 15.2 %all-to-all-start.2 = ((f32[1,2,64,5]{3,1,0,2:T(2,128)}), f32[1,2,64,5]{3,1,0,2:T(2,128)S(1)}, u32[]{:S(2)}, u32[]{:S(2)}) async-start(f32[1,2,64,5]{3,1,0,2:T(2,128)} %copy.140), calls=%async_computation.2 | async-start | bytes 131072 | tf_op jit(solution)/shard_map/all_to_all | solution.py:121
  263.2 14.7 %copy-start.3 = (bf16[128,1,5,128]{0,3,2,1:T(8,128)(2,1)S(1)}, bf16[128,1,5,128]{0,3,2,1:T(8,128)(2,1)}, u32[]{:S(2)}) copy-start(bf16[128,1,5,128]{0,3,2,1:T(8,128)(2,1)} %copy-done.2) | copy-start | bytes 491524
  272.3 16.9 %all-to-all-start.3 = ((f32[1,2,64,640]{3,1,0,2:T(2,128)}), f32[1,2,64,640]{3,1,0,2:T(2,128)S(1)}, u32[]{:S(2)}, u32[]{:S(2)}) async-start(f32[1,2,64,640]{3,1,0,2:T(2,128)} %reshape.241), calls=%async_computation.3 | async-start | bytes 655360 | tf_op jit(solution)/shard_map/all_to_all | solution.py:114
Sparse Core Ops, SparseCore 0:
  27.5 39.5 all-gather.1
